TPU v7x, 32 devices: a whole 2x2x4 slice. The times are simulated.
32 devices in a mesh: row: 4 (over y, core), col: 8 (over z, x).
Axes of the slice: x: 2, y: 2, z: 4, core: 2. Of those that a mesh axis runs over, the one named last changes fastest.
Arguments:
- inputs: bfloat16 [512, 12288], P('col', 'row'), may hold values from -6 to 6
- grad_out: bfloat16 [512, 12288], P('col', 'row'), may hold values from -6 to 6
- w_in: bfloat16 [12288, 24576], P('row', 'col'), may hold values from -0.0546875 to 0.0546875
- w_out: bfloat16 [24576, 12288], P('col', 'row'), may hold values from -0.0390625 to 0.0390625
Outputs:
- outputs: bfloat16 [512, 12288], P('col', 'row')
- grad_in: bfloat16 [512, 12288], P('col', 'row')
- grad_w_in: bfloat16 [12288, 24576], P('row', 'col')
- grad_w_out: bfloat16 [24576, 12288], P('col', 'row')
All inputs are finite; a program needn't handle non-finite values.
Results may differ from a plain program's by a relative error of at most 0.019.
Values may be sent and summed in bfloat16 or wider, within the bound.
A program may use at most 192 MiB of HBM per device.

v0:
```python
from functools import partial
import jax
import jax.numpy as jnp
from jax import lax
from jax.sharding import PartitionSpec as P


def col_panel(values):
    return lax.all_gather(values, "col", axis=0, tiled=True)


def contract(left, right, dims):
    return lax.dot_general(
        left, right, ((dims[0], dims[1]), ((), ())), preferred_element_type=jnp.float32
    )


def row_sums(left, right, dims):
    return lax.psum_scatter(
        contract(left, right, dims).astype(jnp.bfloat16), "row", scatter_dimension=0, tiled=True
    ).astype(jnp.float32)


def row_spread(values):
    return lax.all_gather(values, "row", axis=0, tiled=True)


def col_sums(left, right, dims):
    return lax.psum_scatter(
        contract(
            lax.dynamic_slice_in_dim(
                left, jnp.int32(0), left.shape[0] // lax.axis_size("col") * lax.axis_size("col"), 0
            ),
            right,
            dims,
        ).astype(jnp.bfloat16),
        "col",
        scatter_dimension=0,
        tiled=True,
    ).astype(jnp.float32)


def local(inputs, grad_out, w_in, w_out):
    gelu_tanh = partial(jax.nn.gelu, approximate=True)
    input_all = col_panel(inputs)
    cotan_all = None
    hidden_pre = row_sums(input_all, w_in, ((1,), (0,)))
    act_all = row_spread(gelu_tanh(hidden_pre).astype(jnp.bfloat16))
    outputs = col_sums(act_all, w_out, ((1,), (0,))).astype(jnp.bfloat16)
    cotan_all = col_panel(grad_out)
    grad_act = row_sums(cotan_all, w_out, ((1,), (1,)))
    grad_pre = jax.vjp(gelu_tanh, hidden_pre)[1](grad_act)[0].astype(jnp.bfloat16)
    grad_pre_all = row_spread(grad_pre)
    grad_w_out = contract(act_all, cotan_all, ((0,), (0,))).astype(jnp.bfloat16)
    grad_w_in = contract(input_all, grad_pre_all, ((0,), (0,))).astype(jnp.bfloat16)
    grad_in = col_sums(grad_pre_all, w_in, ((1,), (1,))).astype(jnp.bfloat16)
    return (outputs, grad_in, grad_w_in, grad_w_out)


def solution(mesh):
    placed = (P("col", "row"), P("col", "row"), P("row", "col"), P("col", "row"))
    return jax.shard_map(
        local,
        mesh=mesh,
        in_specs=placed,
        out_specs=(P("col", "row"), P("col", "row"), P("row", "col"), P("col", "row")),
        check_vma=False,
    )
```

profile of v0, /device:TPU:0, one launch (start us, length us, event | category | flops | bytes accessed | tf_op | source)
XLA Modules:
  0.0 441.4 jit_solution(10468758725500619523)
XLA Ops:
  7.2 0.7 all-gather.9.cloned.1.call-update
  7.9 0.7 all-gather.5.cloned.1.call-update
  8.7 64.7 %all-gather.9.cloned.1.call-done = bf16[512,3072]{1,0:T(8,128)(2,1)} async-done(((bf16[64,3072]{1,0:T(8,128)(2,1)}), bf16[512,3072]{1,0:T(8,128)(2,1)}) %all-gather.9.cloned.1.call-update) | async-done | bytes 3145744 | tf_op jit(solution)/shard_map/all_gather | solution.py:9
  73.4 15.9 %convolution_convert_fusion.2 = bf16[512,3072]{1,0:T(8,128)(2,1)} fusion(bf16[512,3072]{1,0:T(8,128)(2,1)} %all-gather.9.cloned.1.call-done, bf16[3072,3072]{1,0:T(8,128)(2,1)} %param.7), kind=kOutput, calls=%fused_computation.3 | convolution fusion | flops 9665249280 | bytes 25165824 | tf_op jit(solution)/shard_map/dot_general | solution.py:13
  89.3 0.0 reduce-scatter.5.cloned.1.call-start
  89.3 45.4 %all-gather.5.cloned.1.call-done = bf16[512,3072]{1,0:T(8,128)(2,1)} async-done(((bf16[64,3072]{1,0:T(8,128)(2,1)}), bf16[512,3072]{1,0:T(8,128)(2,1)}) %all-gather.5.cloned.1.call-update) | async-done | bytes 3145744 | tf_op jit(solution)/shard_map/all_gather | solution.py:9
  134.7 15.8 %convolution_convert_fusion.4 = bf16[512,3072]{1,0:T(8,128)(2,1)} fusion(bf16[512,3072]{1,0:T(8,128)(2,1)} %all-gather.5.cloned.1.call-done, bf16[3072,3072]{1,0:T(8,128)(2,1)} %param.6), kind=kOutput, calls=%fused_computation.5 | convolution fusion | flops 9665249280 | bytes 25165824 | tf_op jit(solution)/shard_map/dot_general | solution.py:13
  150.5 0.0 all-gather.7.cloned.1.call-start
  150.5 23.9 %reduce-scatter.9.cloned.1.call-done = bf16[128,3072]{1,0:T(8,128)(2,1)} async-done(((bf16[512,3072]{1,0:T(8,128)(2,1)}), bf16[128,3072]{1,0:T(8,128)(2,1)}) %reduce-scatter.9.cloned.1.call-update) | async-done | bytes 786448 | tf_op jit(solution)/shard_map/reduce_scatter | solution.py:19
  174.4 41.1 %reduce-scatter.5.cloned.1.call-done = bf16[128,3072]{1,0:T(8,128)(2,1)} async-done(((bf16[512,3072]{1,0:T(8,128)(2,1)}), bf16[128,3072]{1,0:T(8,128)(2,1)}) %reduce-scatter.5.cloned.1.call-update) | async-done | bytes 786448 | tf_op jit(solution)/shard_map/reduce_scatter | solution.py:19
  215.5 3.7 fusion.3
  219.3 0.0 all-gather.11.cloned.1.call-start
  219.3 0.5 all-gather.11.cloned.1.call-update
  219.9 28.1 %all-gather.7.cloned.1.call-done = bf16[512,3072]{1,0:T(8,128)(2,1)} async-done(((bf16[128,3072]{1,0:T(8,128)(2,1)}), bf16[512,3072]{1,0:T(8,128)(2,1)}) %all-gather.7.cloned.1.call-update) | async-done | bytes 3145744 | tf_op jit(solution)/shard_map/all_gather | solution.py:25
  248.0 15.8 %convolution_convert_fusion.3 = bf16[512,3072]{1,0:T(8,128)(2,1)} fusion(bf16[512,3072]{1,0:T(8,128)(2,1)} %all-gather.7.cloned.1.call-done, bf16[3072,3072]{1,0:T(8,128)(2,1)} %param.7), kind=kOutput, calls=%fused_computation.4 | convolution fusion | flops 9665249280 | bytes 25165824 | tf_op jit(solution)/shard_map/dot_general | solution.py:13
  263.8 0.2 reduce-scatter.11.cloned.1.call-start
  264.0 14.5 %all-gather.11.cloned.1.call-done = bf16[512,3072]{1,0:T(8,128)(2,1)} async-done(((bf16[128,3072]{1,0:T(8,128)(2,1)}), bf16[512,3072]{1,0:T(8,128)(2,1)}) %all-gather.11.cloned.1.call-update) | async-done | bytes 3145744 | tf_op jit(solution)/shard_map/all_gather | solution.py:25
  278.5 15.9 %convolution_convert_fusion.1 = bf16[512,3072]{1,0:T(8,128)(2,1)} fusion(bf16[512,3072]{1,0:T(8,128)(2,1)} %all-gather.11.cloned.1.call-done, bf16[3072,3072]{1,0:T(8,128)(2,1)} %param.6), kind=kOutput, calls=%fused_computation.2 | convolution fusion | flops 9665249280 | bytes 25165824 | tf_op jit(solution)/shard_map/dot_general | solution.py:13
  294.5 1.9 copy-done.1
  296.4 15.1 %convert_bitcast_fusion = bf16[3072,3072]{0,1:T(8,128)(2,1)} fusion(bf16[512,3072]{1,0:T(8,128)(2,1)} %all-gather.11.cloned.1.call-done, bf16[512,3072]{1,0:T(8,128)(2,1)S(1)} %copy-done.1), kind=kOutput, calls=%fused_computation | convolution fusion | flops 9673113600 | bytes 25165824 | tf_op jit(solution)/shard_map/dot_general | solution.py:13
  311.5 24.8 %copy.8 = bf16[3072,3072]{1,0:T(8,128)(2,1)} copy(bf16[3072,3072]{0,1:T(8,128)(2,1)} %convert_bitcast_fusion) | data formatting | bytes 37748736
  336.3 15.0 %convolution_convert_fusion = bf16[3072,3072]{1,0:T(8,128)(2,1)} fusion(bf16[512,3072]{1,0:T(8,128)(2,1)} %all-gather.7.cloned.1.call-done, bf16[512,3072]{1,0:T(8,128)(2,1)S(1)} %copy-done), kind=kOutput, calls=%fused_computation.1 | convolution fusion | flops 9673113600 | bytes 25165824 | tf_op jit(solution)/shard_map/dot_general | solution.py:13
  351.3 5.6 %reduce-scatter.7.cloned.1.call-done = bf16[64,3072]{1,0:T(8,128)(2,1)} async-done(((bf16[512,3072]{1,0:T(8,128)(2,1)}), bf16[64,3072]{1,0:T(8,128)(2,1)}) %reduce-scatter.7.cloned.1.call-update) | async-done | bytes 393232 | tf_op jit(solution)/shard_map/reduce_scatter | solution.py:29
  356.9 77.6 %reduce-scatter.11.cloned.1.call-done = bf16[64,3072]{1,0:T(8,128)(2,1)} async-done(((bf16[512,3072]{1,0:T(8,128)(2,1)}), bf16[64,3072]{1,0:T(8,128)(2,1)}) %reduce-scatter.11.cloned.1.call-update) | async-done | bytes 393232 | tf_op jit(solution)/shard_map/reduce_scatter | solution.py:29
  (12 shorter events, 0.2 us)
Async XLA Ops:
  7.2 66.2 %all-gather.9.cloned.1.call-start = ((), (), s32[]{:S(2)}) async-start(), calls=%async_computation.8 | async-start | bytes 3538944 | tf_op jit(solution)/shard_map/all_gather | solution.py:9
  7.9 126.8 %all-gather.5.cloned.1.call-start = ((), (), s32[]{:S(2)}) async-start(), calls=%async_computation.4 | async-start | bytes 3538944 | tf_op jit(solution)/shard_map/all_gather | solution.py:9
  8.6 165.7 %reduce-scatter.9.cloned.1.call-start = ((), (), s32[]{:S(2)}) async-start(), calls=%async_computation.9 | async-start | bytes 3932160 | tf_op jit(solution)/shard_map/reduce_scatter | solution.py:19
  89.3 126.2 %reduce-scatter.5.cloned.1.call-start = ((), (), s32[]{:S(2)}) async-start(), calls=%async_computation.5 | async-start | bytes 3932160 | tf_op jit(solution)/shard_map/reduce_scatter | solution.py:19
  150.5 97.5 %all-gather.7.cloned.1.call-start = ((), (), s32[]{:S(2)}) async-start(), calls=%async_computation.6 | async-start | bytes 3932160 | tf_op jit(solution)/shard_map/all_gather | solution.py:25
  219.3 59.3 %all-gather.11.cloned.1.call-start = ((), (), s32[]{:S(2)}) async-start(), calls=%async_computation.10 | async-start | bytes 3932160 | tf_op jit(solution)/shard_map/all_gather | solution.py:25
  219.8 137.1 %reduce-scatter.7.cloned.1.call-start = ((), (), s32[]{:S(2)}) async-start(), calls=%async_computation.7 | async-start | bytes 3538944 | tf_op jit(solution)/shard_map/reduce_scatter | solution.py:29
  263.8 170.7 %reduce-scatter.11.cloned.1.call-start = ((), (), s32[]{:S(2)}) async-start(), calls=%async_computation.11 | async-start | bytes 3538944 | tf_op jit(solution)/shard_map/reduce_scatter | solution.py:29
  294.5 1.9 copy-start.1
  311.5 24.8 %copy-start = (bf16[512,3072]{1,0:T(8,128)(2,1)S(1)}, bf16[512,3072]{1,0:T(8,128)(2,1)}, u32[]{:S(2)}) copy-start(bf16[512,3072]{1,0:T(8,128)(2,1)} %all-gather.9.cloned.1.call-done) | copy-start | bytes 9437188
Sparse Core Ops, SparseCore 0:
  10.2 63.1 all-gather.8
  75.5 59.0 all-gather.4
  137.8 36.5 reduce-scatter.8
  177.5 37.9 reduce-scatter.4
  219.4 28.5 all-gather.6
  249.9 28.5 all-gather.10
  282.7 74.2 reduce-scatter.6
  361.1 73.3 reduce-scatter.10
where the time goes:
time: 442 us; the launch traced here: 441 us
  waiting for transfers between devices  303 us (69%)
  matrix products  93.5 us (21%)
  local copies, waits for them, and re-layouts  26.7 us (6%)
  between operations  14.1 us (3%)
    all_gather x2, waiting for transfers between devices, col_panel(): return lax.all_gather(values, 'col', axis=0, tiled=True)  110 us
    dot_general x6, matrix products, contract(): lax.dot_general(left, right, ((dims[0], dims[1]), ((), ())), preferred_el...  93.5 us
    reduce_scatter x2, waiting for transfers between devices, col_sums(): lax.psum_scatter(contract(lax.dynamic_slice_in_dim(left, jnp.int32(0), le...  83.2 us
    reduce_scatter x2, waiting for transfers between devices, row_sums(): lax.psum_scatter(contract(left, right, dims).astype(jnp.bfloat16), 'row',...  65 us
    all_gather x2, waiting for transfers between devices, row_spread(): return lax.all_gather(values, 'row', axis=0, tiled=True)  42.5 us
    unnamed x5, local copies, waits for them, and re-layouts  26.7 us
  transfers between devices with their start and end apart: 8, of which 8 were waited for; matrix products, arithmetic and copies ran while one was open for 27% of the time, Pallas kernels for 0%

commit v1 on v0

--- a/solution.py
+++ b/solution.py
@@ -1,8 +1,39 @@
+import functools
 from functools import partial
 import jax
 import jax.numpy as jnp
 from jax import lax
 from jax.sharding import PartitionSpec as P
+
+
+def pass_the_rates(block_in, mesh_name):
+    near = lax.axis_size(mesh_name)
+    step_out = lax.axis_index(mesh_name)
+    seen_now, current_block, newest = (near, step_out, block_in.shape[0])
+    entries = [m * seen_now if ix == 0 else m for ix, m in enumerate(block_in.shape)]
+    formed = jnp.zeros(entries, block_in.dtype)
+    new = lax.dynamic_update_slice_in_dim(formed, block_in, current_block * newest, axis=0)
+    out_arr = carry_out = block_in
+    rr = 1
+    while rr < seen_now // 2 + 1:
+        out_arr = lax.ppermute(
+            out_arr, mesh_name, [(ix, (ix + 1) % seen_now) for ix in range(seen_now)]
+        )
+        new = lax.dynamic_update_slice_in_dim(
+            new, out_arr, (current_block - rr) % seen_now * newest, axis=0
+        )
+        if 2 * rr < seen_now:
+            carry_out = lax.ppermute(
+                carry_out, mesh_name, [(ix, (ix - 1) % seen_now) for ix in range(seen_now)]
+            )
+            new = lax.dynamic_update_slice_in_dim(
+                new, carry_out, (current_block + rr) % seen_now * newest, axis=0
+            )
+        rr += 1
+    return new
+
+
+advance_field = functools.partial(pass_the_rates, mesh_name="row")
 
 
 def col_panel(values):
@@ -22,7 +53,7 @@
 
 
 def row_spread(values):
-    return lax.all_gather(values, "row", axis=0, tiled=True)
+    return advance_field(values)
 
 
 def col_sums(left, right, dims):

time: 442 us -> 399 us (0.903)
  waiting for transfers between devices: 303 us -> 253 us
  local copies, waits for them, and re-layouts: 26.7 us -> 31.9 us
    ppermute x0 -> x6, waiting for transfers between devices: none -> 72.3 us  [the longest x4 72.3 us: pass_the_rates(): lax.ppermute(out_arr, mesh_name, [(ix, (ix + 1) % seen_now) for ix in ran...]
    all_gather x2 -> x0, waiting for transfers between devices: 42.5 us -> none  [row_spread(): return lax.all_gather(values, 'row', axis=0, tiled=True)]
    reduce_scatter x2, waiting for transfers between devices: 65 us -> 23.8 us  [row_sums(): lax.psum_scatter(contract(left, right, dims).astype(jnp.bfloat16), 'row',...]
    reduce_scatter x2, waiting for transfers between devices: 83.2 us -> 45.1 us  [col_sums(): lax.psum_scatter(contract(lax.dynamic_slice_in_dim(left, jnp.int32(0), le...]
    unnamed x5 -> x13, local copies, waits for them, and re-layouts: 26.7 us -> 30.7 us
  transfers between devices with their start and end apart: 8 -> 12, of which waited for: 8 -> 8; matrix products, arithmetic and copies ran while one was open for 27% -> 30% of each run, Pallas kernels for 0% -> 0%
where the time goes in v1:
time: 399 us; the launch traced here: 398 us
  waiting for transfers between devices  253 us (63%)
  matrix products  92 us (23%)
  local copies, waits for them, and re-layouts  31.9 us (8%)
  between operations  14.3 us (4%)
    all_gather x2, waiting for transfers between devices, col_panel(): return lax.all_gather(values, 'col', axis=0, tiled=True)  110 us
    dot_general x6, matrix products, contract(): lax.dot_general(left, right, ((dims[0], dims[1]), ((), ())), preferred_el...  92 us
    ppermute x4, waiting for transfers between devices, pass_the_rates(): lax.ppermute(out_arr, mesh_name, [(ix, (ix + 1) % seen_now) for ix in ran...  72.3 us
    reduce_scatter x2, waiting for transfers between devices, col_sums(): lax.psum_scatter(contract(lax.dynamic_slice_in_dim(left, jnp.int32(0), le...  45.1 us
    unnamed x13, local copies, waits for them, and re-layouts  30.7 us
    reduce_scatter x2, waiting for transfers between devices, row_sums(): lax.psum_scatter(contract(left, right, dims).astype(jnp.bfloat16), 'row',...  23.8 us
  transfers between devices with their start and end apart: 12, of which 8 were waited for; matrix products, arithmetic and copies ran while one was open for 30% of the time, Pallas kernels for 0%

profile of v1, /device:TPU:0, one launch (start us, length us, event | category | flops | bytes accessed | tf_op | source)
XLA Modules:
  0.0 398.3 jit_solution(5835694062178043810)
XLA Ops:
  7.9 0.7 all-gather.5.cloned.1.call-update
  8.7 64.7 %all-gather.3.cloned.1.call-done = bf16[512,3072]{1,0:T(8,128)(2,1)} async-done(((bf16[64,3072]{1,0:T(8,128)(2,1)}), bf16[512,3072]{1,0:T(8,128)(2,1)}) %all-gather.3.cloned.1.call-update) | async-done | bytes 3145744 | tf_op jit(solution)/shard_map/all_gather | solution.py:40
  73.4 15.8 %convolution_convert_fusion.4 = bf16[512,3072]{1,0:T(8,128)(2,1)} fusion(bf16[512,3072]{1,0:T(8,128)(2,1)} %all-gather.3.cloned.1.call-done, bf16[3072,3072]{1,0:T(8,128)(2,1)} %param.6), kind=kOutput, calls=%fused_computation.5 | convolution fusion | flops 9665249280 | bytes 25165824 | tf_op jit(solution)/shard_map/dot_general | solution.py:44
  89.2 45.4 %all-gather.5.cloned.1.call-done = bf16[512,3072]{1,0:T(8,128)(2,1)} async-done(((bf16[64,3072]{1,0:T(8,128)(2,1)}), bf16[512,3072]{1,0:T(8,128)(2,1)}) %all-gather.5.cloned.1.call-update) | async-done | bytes 3145744 | tf_op jit(solution)/shard_map/all_gather | solution.py:40
  134.7 15.9 %convolution_convert_fusion.2 = bf16[512,3072]{1,0:T(8,128)(2,1)} fusion(bf16[512,3072]{1,0:T(8,128)(2,1)} %all-gather.5.cloned.1.call-done, bf16[3072,3072]{1,0:T(8,128)(2,1)} %param.7), kind=kOutput, calls=%fused_computation.3 | convolution fusion | flops 9665249280 | bytes 25165824 | tf_op jit(solution)/shard_map/dot_general | solution.py:44
  150.6 23.8 %reduce-scatter.5.cloned.1.call-done = bf16[128,3072]{1,0:T(8,128)(2,1)} async-done(((bf16[512,3072]{1,0:T(8,128)(2,1)}), bf16[128,3072]{1,0:T(8,128)(2,1)}) %reduce-scatter.5.cloned.1.call-update) | async-done | bytes 786448 | tf_op jit(solution)/shard_map/reduce_scatter | solution.py:50
  174.4 1.7 fusion.8
  176.3 1.7 collective-permute-start.1
  177.9 17.5 %collective-permute-done = bf16[128,3072]{1,0:T(8,128)(2,1)S(1)} collective-permute-done((bf16[128,3072]{1,0:T(8,128)(2,1)S(1)}, bf16[128,3072]{1,0:T(8,128)(2,1)S(1)}, u32[]{:S(2)}, u32[]{:S(2)}) %collective-permute-start) | collective-permute-done | bytes 786464 | tf_op jit(solution)/shard_map/ppermute | solution.py:19
  196.6 26.0 %collective-permute-done.2 = bf16[128,3072]{1,0:T(8,128)(2,1)S(1)} collective-permute-done((bf16[128,3072]{1,0:T(8,128)(2,1)S(1)}, bf16[128,3072]{1,0:T(8,128)(2,1)S(1)}, u32[]{:S(2)}, u32[]{:S(2)}) %collective-permute-start.2) | collective-permute-done | bytes 786464 | tf_op jit(solution)/shard_map/ppermute | solution.py:19
  222.7 1.6 copy-done.3
  224.4 15.0 %convolution_convert_fusion.3 = bf16[512,3072]{1,0:T(8,128)(2,1)} fusion(bf16[512,3072]{1,0:T(8,128)(2,1)S(1)} %constant_dynamic-update-slice_fusion.4, bf16[3072,3072]{1,0:T(8,128)(2,1)} %param.7), kind=kOutput, calls=%fused_computation.4 | convolution fusion | flops 9665249280 | bytes 25165824 | tf_op jit(solution)/shard_map/dot_general | solution.py:44
  239.9 0.7 copy-done.5
  240.6 1.2 constant_dynamic-update-slice_fusion.3
  241.9 1.7 collective-permute-start.4
  243.6 17.5 %collective-permute-done.3 = bf16[128,3072]{1,0:T(8,128)(2,1)S(1)} collective-permute-done((bf16[128,3072]{1,0:T(8,128)(2,1)S(1)}, bf16[128,3072]{1,0:T(8,128)(2,1)S(1)}, u32[]{:S(2)}, u32[]{:S(2)}) %collective-permute-start.3) | collective-permute-done | bytes 786464 | tf_op jit(solution)/shard_map/ppermute | solution.py:19
  261.3 11.2 %collective-permute-done.5 = bf16[128,3072]{1,0:T(8,128)(2,1)S(1)} collective-permute-done((bf16[128,3072]{1,0:T(8,128)(2,1)S(1)}, bf16[128,3072]{1,0:T(8,128)(2,1)S(1)}, u32[]{:S(2)}, u32[]{:S(2)}) %collective-permute-start.5) | collective-permute-done | bytes 786464 | tf_op jit(solution)/shard_map/ppermute | solution.py:19
  272.6 1.7 copy-done.1
  274.3 15.2 %convolution_convert_fusion.1 = bf16[512,3072]{1,0:T(8,128)(2,1)} fusion(bf16[512,3072]{1,0:T(8,128)(2,1)S(1)} %constant_dynamic-update-slice_fusion, bf16[3072,3072]{1,0:T(8,128)(2,1)} %param.6), kind=kOutput, calls=%fused_computation.2 | convolution fusion | flops 9665249280 | bytes 25165824 | tf_op jit(solution)/shard_map/dot_general | solution.py:44
  289.5 1.9 copy-done.2
  291.4 15.0 %convert_bitcast_fusion = bf16[3072,3072]{0,1:T(8,128)(2,1)} fusion(bf16[512,3072]{1,0:T(8,128)(2,1)S(1)} %copy-done.2, bf16[512,3072]{1,0:T(8,128)(2,1)} %all-gather.3.cloned.1.call-done), kind=kOutput, calls=%fused_computation | convolution fusion | flops 9673113600 | bytes 25165824 | tf_op jit(solution)/shard_map/dot_general | solution.py:44
  306.5 24.8 %copy.8 = bf16[3072,3072]{1,0:T(8,128)(2,1)} copy(bf16[3072,3072]{0,1:T(8,128)(2,1)} %convert_bitcast_fusion) | data formatting | bytes 37748736
  331.2 15.1 %convolution_convert_fusion = bf16[3072,3072]{1,0:T(8,128)(2,1)} fusion(bf16[512,3072]{1,0:T(8,128)(2,1)S(1)} %copy-done.4, bf16[512,3072]{1,0:T(8,128)(2,1)} %all-gather.5.cloned.1.call-done), kind=kOutput, calls=%fused_computation.1 | convolution fusion | flops 9673113600 | bytes 25165824 | tf_op jit(solution)/shard_map/dot_general | solution.py:44
  346.3 45.1 %reduce-scatter.11.cloned.1.call-done = bf16[64,3072]{1,0:T(8,128)(2,1)} async-done(((bf16[512,3072]{1,0:T(8,128)(2,1)}), bf16[64,3072]{1,0:T(8,128)(2,1)}) %reduce-scatter.11.cloned.1.call-update) | async-done | bytes 393232 | tf_op jit(solution)/shard_map/reduce_scatter | solution.py:60
  (36 shorter events, 2.9 us)
Async XLA Ops:
  7.2 66.2 %all-gather.3.cloned.1.call-start = ((), (), s32[]{:S(2)}) async-start(), calls=%async_computation.4 | async-start | bytes 3538944 | tf_op jit(solution)/shard_map/all_gather | solution.py:40
  7.9 126.8 %all-gather.5.cloned.1.call-start = ((), (), s32[]{:S(2)}) async-start(), calls=%async_computation.7 | async-start | bytes 3538944 | tf_op jit(solution)/shard_map/all_gather | solution.py:40
  8.6 165.7 %reduce-scatter.5.cloned.1.call-start = ((), (), s32[]{:S(2)}) async-start(), calls=%async_computation.5 | async-start | bytes 3932160 | tf_op jit(solution)/shard_map/reduce_scatter | solution.py:50
  89.2 150.3 %reduce-scatter.9.cloned.1.call-start = ((), (), s32[]{:S(2)}) async-start(), calls=%async_computation.8 | async-start | bytes 3932160 | tf_op jit(solution)/shard_map/reduce_scatter | solution.py:50
  150.5 195.8 %reduce-scatter.7.cloned.1.call-start = ((), (), s32[]{:S(2)}) async-start(), calls=%async_computation.6 | async-start | bytes 3538944 | tf_op jit(solution)/shard_map/reduce_scatter | solution.py:60
  174.4 21.5 %copy-start = (bf16[128,3072]{1,0:T(8,128)(2,1)S(1)}, bf16[128,3072]{1,0:T(8,128)(2,1)}, u32[]{:S(2)}) copy-start(bf16[128,3072]{1,0:T(8,128)(2,1)} %reduce-scatter.5.cloned.1.call-done) | copy-start | bytes 2359300
  176.1 19.3 %collective-permute-start = (bf16[128,3072]{1,0:T(8,128)(2,1)S(1)}, bf16[128,3072]{1,0:T(8,128)(2,1)S(1)}, u32[]{:S(2)}, u32[]{:S(2)}) collective-permute-start(bf16[128,3072]{1,0:T(8,128)(2,1)S(1)} %fusion.8), channel_id=1, source_target_pairs={{0,8},{8,16},{16,24},{24,0},{1,9},{9,17},{17,25},{25,1},{2,10},{10... | collective-permute-start | bytes 2359304 | tf_op jit(solution)/shard_map/ppermute | solution.py:19
  176.3 20.3 %collective-permute-start.1 = (bf16[128,3072]{1,0:T(8,128)(2,1)S(1)}, bf16[128,3072]{1,0:T(8,128)(2,1)S(1)}, u32[]{:S(2)}, u32[]{:S(2)}) collective-permute-start(bf16[128,3072]{1,0:T(8,128)(2,1)S(1)} %fusion.8), channel_id=1, source_target_pairs={{0,24},{8,0},{16,8},{24,16},{1,25},{9,1},{17,9},{25,17},{2,26},{10... | collective-permute-start | bytes 2359304 | tf_op jit(solution)/shard_map/ppermute | solution.py:26
  195.5 27.2 %collective-permute-start.2 = (bf16[128,3072]{1,0:T(8,128)(2,1)S(1)}, bf16[128,3072]{1,0:T(8,128)(2,1)S(1)}, u32[]{:S(2)}, u32[]{:S(2)}) collective-permute-start(bf16[128,3072]{1,0:T(8,128)(2,1)S(1)} %collective-permute-done), channel_id=1, source_target_pairs={{0,8},{8,16},{16,24},{24,0},{1,9},{9,17},{17,25},{25,1},{2,10},{10... | collective-permute-start | bytes 2359304 | tf_op jit(solution)/shard_map/ppermute | solution.py:19
  222.7 1.6 copy-start.3
  239.4 152.0 %reduce-scatter.11.cloned.1.call-start = ((), (), s32[]{:S(2)}) async-start(), calls=%async_computation.9 | async-start | bytes 3538944 | tf_op jit(solution)/shard_map/reduce_scatter | solution.py:60
  239.5 1.1 copy-start.5
  241.8 19.3 %collective-permute-start.3 = (bf16[128,3072]{1,0:T(8,128)(2,1)S(1)}, bf16[128,3072]{1,0:T(8,128)(2,1)S(1)}, u32[]{:S(2)}, u32[]{:S(2)}) collective-permute-start(bf16[128,3072]{1,0:T(8,128)(2,1)S(1)} %get-tuple-element.9), channel_id=1, source_target_pairs={{0,8},{8,16},{16,24},{24,0},{1,9},{9,17},{17,25},{25,1},{2,10},{10... | collective-permute-start | bytes 2359304 | tf_op jit(solution)/shard_map/ppermute | solution.py:19
  241.9 19.3 %collective-permute-start.4 = (bf16[128,3072]{1,0:T(8,128)(2,1)S(1)}, bf16[128,3072]{1,0:T(8,128)(2,1)S(1)}, u32[]{:S(2)}, u32[]{:S(2)}) collective-permute-start(bf16[128,3072]{1,0:T(8,128)(2,1)S(1)} %get-tuple-element.9), channel_id=1, source_target_pairs={{0,24},{8,0},{16,8},{24,16},{1,25},{9,1},{17,9},{25,17},{2,26},{10... | collective-permute-start | bytes 2359304 | tf_op jit(solution)/shard_map/ppermute | solution.py:26
  261.1 11.4 %collective-permute-start.5 = (bf16[128,3072]{1,0:T(8,128)(2,1)S(1)}, bf16[128,3072]{1,0:T(8,128)(2,1)S(1)}, u32[]{:S(2)}, u32[]{:S(2)}) collective-permute-start(bf16[128,3072]{1,0:T(8,128)(2,1)S(1)} %collective-permute-done.3), channel_id=1, source_target_pairs={{0,8},{8,16},{16,24},{24,0},{1,9},{9,17},{17,25},{25,1},{2,10},{10... | collective-permute-start | bytes 2359304 | tf_op jit(solution)/shard_map/ppermute | solution.py:19
  272.6 1.7 copy-start.1
  289.5 1.9 copy-start.2
  306.5 24.8 %copy-start.4 = (bf16[512,3072]{1,0:T(8,128)(2,1)S(1)}, bf16[512,3072]{1,0:T(8,128)(2,1)}, u32[]{:S(2)}) copy-start(bf16[512,3072]{1,0:T(8,128)(2,1)} %copy-done.3) | copy-start | bytes 9437188
Sparse Core Ops, SparseCore 0:
  10.2 63.1 all-gather.2
  75.5 59.0 all-gather.4
  137.8 36.5 reduce-scatter.4
  177.5 46.0 reduce-scatter.8
  239.6 74.3 reduce-scatter.6
  317.9 73.4 reduce-scatter.10
